TPU v7x, 128 devices: a whole 4x4x4 slice. The times are simulated.
128 devices in a mesh: seq: 16 (over y, x), exp: 8 (over z, core).
Axes of the slice: x: 4, y: 4, z: 4, core: 2. Of those that a mesh axis runs over, the one named last changes fastest.
Arguments:
- queries: bfloat16 [2048, 8192], P('seq', 'exp'), may hold values from -0.5 to 0.5
- keys: bfloat16 [2048, 8192], P('seq', 'exp'), may hold values from -0.5 to 0.5
- values: bfloat16 [2048, 8192], P('seq', 'exp'), may hold values from -6 to 6
- attn_grad: bfloat16 [2048, 8192], P('seq', 'exp'), may hold values from -6 to 6
- log_decay: float32 [2048, 64], P('seq', 'exp'), may hold values from -0.75 to 0, as said below
- moe_grad: bfloat16 [2048, 6144], P('seq', 'exp'), may hold values from -6 to 6
- gate_probs: bfloat16 [2048, 2], P('seq'), may hold values from 0.099609375 to 0.8984375
- expert_ids: int32 [2048, 2], P('seq'), may hold values from 0 to 7, all different within a row; in each aligned block of 128 rows (0 to 127, 128 to 255, ...) at most 48 rows name the same one
- hidden_acts: bfloat16 [8, 768, 9216], P('exp', None, 'seq'), may hold values from -0.3125 to 0.3125
- down_weight: bfloat16 [8, 9216, 6144], P('exp', 'seq'), may hold values from -0.0625 to 0.0625
Outputs:
- query_grad: bfloat16 [2048, 8192], P('seq', 'exp')
- key_grad: bfloat16 [2048, 8192], P('seq', 'exp')
- value_grad: bfloat16 [2048, 8192], P('seq', 'exp')
- hidden_grad: bfloat16 [8, 768, 9216], P('exp', None, 'seq')
- weight_grad: bfloat16 [8, 9216, 6144], P('exp', 'seq')
- gate_grad: float32 [2048, 2], P('seq')
Inputs may be any that keep to these rules, and one draw needn't show every extreme that they name: `expert_ids`: each row names 2 different experts. In the 128 rows of one index of seq no expert is named by more than 48 rows, and every draw has such a block where some expert is named by exactly 48 rows. `log_decay`: log decay of each head at each position; never positive.
All inputs are finite; a program needn't handle non-finite values.
Results may differ from a plain program's by a relative error of at most 0.005.
Values may be sent and summed in bfloat16 or wider, within the bound.
A program may use at most 128 MiB of HBM per device.

v0:
```python
import jax
import jax.numpy as jnp
from jax import lax
from jax.sharding import PartitionSpec as P

precise = lax.Precision.HIGHEST


def prefix(part, axis, combine, identity, reverse):
    count = lax.axis_size(axis)
    place = lax.axis_index(axis)
    ahead = count - 1 - place if reverse else place
    gathered = jax.tree.map(lambda a: lax.all_gather(a, axis), part)
    state = jax.tree.map(lambda a, e: jnp.zeros_like(a) + jnp.asarray(e, a.dtype), part, identity)

    def one(lap, state):
        source = count - 1 - lap if reverse else lap
        return combine(
            state, jax.tree.map(lambda a: lax.dynamic_index_in_dim(a, source, 0, False), gathered)
        )

    return lax.fori_loop(0, ahead, one, state)


def chain_combine(earlier, latter):
    return (jnp.exp(latter[1])[:, None, None] * earlier[0] + latter[0], earlier[1] + latter[1])


def on_device(
    queries,
    keys,
    values,
    attn_grad,
    log_decay,
    moe_grad,
    gate_probs,
    expert_ids,
    hidden_acts,
    down_weight,
):
    tok_count = queries.shape[0]
    head_count = log_decay.shape[1]
    head_width = queries.shape[1] // head_count
    shaped = (tok_count, head_count, head_width)
    query_f = queries.astype(jnp.float32).reshape(shaped)
    key_f = keys.astype(jnp.float32).reshape(shaped)
    value_f = values.astype(jnp.float32).reshape(shaped)
    grad_f = attn_grad.astype(jnp.float32).reshape(shaped)
    cumul = jnp.cumsum(log_decay, axis=0)
    total = cumul[-1]
    tail_w = jnp.exp(total[None, :] - cumul)
    lead_w = jnp.exp(cumul)
    state_kv = jnp.einsum("th,thi,thj->hij", tail_w, key_f, value_f, precision=precise)
    state_qg = jnp.einsum("th,thi,thj->hij", lead_w, query_f, grad_f, precision=precise)
    zero_state = jnp.zeros_like(state_kv)
    zero_gain = jnp.zeros_like(total)
    incoming = prefix((state_kv, total), "seq", chain_combine, (zero_state, zero_gain), False)[0]
    upcoming = prefix((state_qg, total), "seq", chain_combine, (zero_state, zero_gain), True)[0]
    causal = jnp.arange(tok_count)[:, None] >= jnp.arange(tok_count)[None, :]
    spread = cumul.T[:, :, None] - cumul.T[:, None, :]
    decay_mask = jnp.exp(jnp.where(causal[None], spread, -jnp.inf))
    grad_scores = jnp.einsum("thj,shj->hts", grad_f, value_f, precision=precise) * decay_mask
    qk_scores = jnp.einsum("thi,shi->hts", query_f, key_f, precision=precise) * decay_mask
    query_g = jnp.einsum("hts,shi->thi", grad_scores, key_f, precision=precise)
    query_g = query_g + lead_w[:, :, None] * jnp.einsum(
        "thj,hij->thi", grad_f, incoming, precision=precise
    )
    key_g = jnp.einsum("hts,thi->shi", grad_scores, query_f, precision=precise)
    key_g = key_g + tail_w[:, :, None] * jnp.einsum(
        "shj,hij->shi", value_f, upcoming, precision=precise
    )
    value_g = jnp.einsum("hts,thj->shj", qk_scores, grad_f, precision=precise)
    value_g = value_g + tail_w[:, :, None] * jnp.einsum(
        "shi,hij->shj", key_f, upcoming, precision=precise
    )
    flat_width = head_count * head_width
    query_grad = query_g.reshape(tok_count, flat_width).astype(jnp.bfloat16)
    key_grad = key_g.reshape(tok_count, flat_width).astype(jnp.bfloat16)
    value_grad = value_g.reshape(tok_count, flat_width).astype(jnp.bfloat16)
    expert_here = lax.axis_index("exp")
    cap_size = hidden_acts.shape[1] // lax.axis_size("seq")
    chosen_here = expert_ids == expert_here
    routed = jnp.any(chosen_here, axis=1)
    token_gate = jnp.sum(jnp.where(chosen_here, gate_probs.astype(jnp.float32), 0.0), axis=1)
    slot_rank = jnp.cumsum(routed.astype(jnp.int32)) - 1
    slot_ids = jnp.arange(cap_size, dtype=jnp.int32)
    selector = ((slot_rank[None, :] == slot_ids[:, None]) & routed[None, :]).astype(jnp.float32)
    slot_gate = jnp.dot(selector, token_gate, precision=precise).astype(jnp.bfloat16)
    whole_rows = lax.all_gather(moe_grad, "exp", axis=1, tiled=True)
    slot_rows = jnp.dot(
        selector.astype(jnp.bfloat16), whole_rows, preferred_element_type=jnp.float32
    ).astype(jnp.bfloat16)
    weight_here = down_weight[0]
    hidden_here = hidden_acts[0]
    piece_rows = lax.all_gather(slot_rows, "seq", axis=0, tiled=True)
    piece_gate = lax.all_gather(slot_gate, "seq", axis=0, tiled=True)
    back_rows = lax.dot_general(
        piece_rows, weight_here, (((1,), (1,)), ((), ())), preferred_element_type=jnp.float32
    )
    gate_col = piece_gate.astype(jnp.float32)[:, None]
    hidden_out = (gate_col * back_rows).astype(jnp.bfloat16)
    piece_parts = jnp.sum(back_rows * hidden_here.astype(jnp.float32), axis=1)
    slot_parts = piece_parts
    weighted = (gate_col * piece_rows.astype(jnp.float32)).astype(jnp.bfloat16)
    grad_sum = lax.dot_general(
        hidden_here, weighted, (((0,), (0,)), ((), ())), preferred_element_type=jnp.float32
    )
    grad_sum, hidden_out, slot_parts = (grad_sum, hidden_out, slot_parts)
    own_parts = lax.psum_scatter(slot_parts, "seq", scatter_dimension=0, tiled=True)
    per_token = jnp.dot(selector.T, own_parts, precision=precise)
    local_gate = jnp.where(chosen_here, per_token[:, None], 0.0)
    gate_grad = lax.psum(local_gate, "exp")
    return (
        query_grad,
        key_grad,
        value_grad,
        hidden_out[None],
        grad_sum.astype(jnp.bfloat16)[None],
        gate_grad,
    )


def solution(mesh):
    return jax.shard_map(
        on_device,
        mesh=mesh,
        in_specs=(
            P("seq", "exp"),
            P("seq", "exp"),
            P("seq", "exp"),
            P("seq", "exp"),
            P("seq", "exp"),
            P("seq", "exp"),
            P("seq", None),
            P("seq", None),
            P("exp", None, "seq"),
            P("exp", "seq", None),
        ),
        out_specs=(
            P("seq", "exp"),
            P("seq", "exp"),
            P("seq", "exp"),
            P("exp", None, "seq"),
            P("exp", "seq", None),
            P("seq", None),
        ),
        check_vma=False,
    )
```

profile of v0, /device:TPU:1, one launch (start us, length us, event | category | flops | bytes accessed | tf_op | source)
XLA Modules:
  0.0 343.7 jit_solution(9725436786065418335)
XLA Ops:
  7.2 0.7 all-gather.8.cloned.1.call-update
  8.0 0.8 copy.64
  8.8 1.1 copy.67
  10.2 1.2 fusion.21
  11.4 1.1 copy.93
  12.6 1.1 copy.74
  13.8 1.5 fusion.18
  15.3 0.7 select_reduce_fusion
  16.5 21.5 %all-gather.8.cloned.1.call-done = bf16[128,6144]{1,0:T(8,128)(2,1)} async-done(((bf16[128,768]{1,0:T(8,128)(2,1)}), bf16[128,6144]{1,0:T(8,128)(2,1)}) %all-gather.8.cloned.1.call-update) | async-done | bytes 1572880 | tf_op jit(solution)/shard_map/all_gather | solution.py:89
  37.9 2.6 convolution_convert_fusion
  40.6 0.6 fusion.44
  41.9 0.2 dynamic-update-slice
  42.1 33.4 %all-reduce = bf16[768]{0:T(1024)(128)(2,1)S(1)} all-reduce(bf16[768]{0:T(1024)(128)(2,1)S(1)} %dynamic-update-slice), channel_id=1, replica_groups=mesh['seq'=16,'exp'=8] {'seq'}, use_global_device_ids=true, to_apply=%add | all-reduce | flops 768 | bytes 3072
  76.2 15.0 %all-gather.2 = f32[16,1,8]{2,1,0:T(1,128)S(1)} all-gather(f32[1,1,8]{2,1,0:T(1,128)S(1)} %get-tuple-element.211), channel_id=1, replica_groups=mesh['seq'=16,'exp'=8] {'seq'}, dimensions={0}, use_global_device_ids=true | all-gather | bytes 544 | tf_op jit(solution)/shard_map/all_gather | solution.py:13
  91.2 0.3 convolution_multiply_fusion.1
  91.5 0.3 convolution_multiply_fusion
  91.9 19.4 %all-gather.12.cloned.1.call-done = f32[128,128,128]{2,1,0:T(8,128)} async-done(((f32[8,128,128]{2,1,0:T(8,128)}), f32[128,128,128]{2,1,0:T(8,128)}) %all-gather.12.cloned.1.call-update) | async-done | bytes 8388624 | tf_op jit(solution)/shard_map/all_gather | solution.py:13
  111.3 0.4 fusion.7
  111.7 0.7 fusion.14
  112.4 0.8 copy.84
  113.2 70.5 %all-gather.14.cloned.1.call-done = f32[128,128,128]{2,1,0:T(8,128)} async-done(((f32[8,128,128]{2,1,0:T(8,128)}), f32[128,128,128]{2,1,0:T(8,128)}) %all-gather.14.cloned.1.call-update) | async-done | bytes 8388624 | tf_op jit(solution)/shard_map/all_gather | solution.py:13
  183.7 18.6 %while.27 = (s32[]{:T(128)}, f32[8,128,128]{2,1,0:T(8,128)S(1)}, s32[]{:T(128)}, f32[16,8]{1,0:T(8,128)S(1)}, f32[16,8,128,128]{3,2,1,0:T(8,128)}, /*index=5*/s32[]{:T(128)}, s32[]{:T(128)}, s32[]{:T(128)}, s32[]{:T(128)}) while((s32[]{:T(128)}, f32[8,128,128]{2,1,0:T(8,128)S(1)}, s32[]{:T(128)}, f32[16,8]{1,0:T(8,128)S(1)}, ...), condition=%wide.region_4.5_spmd, body=%wide.region_3.4_spmd.sunk | while | flops 262150 | bytes 1573115 | solution.py:22
  183.8 1.2 bitcast_add_fusion.5
  185.0 1.2 bitcast_add_fusion.5
  186.2 1.2 bitcast_add_fusion.5
  187.5 1.2 bitcast_add_fusion.5
  188.7 1.2 bitcast_add_fusion.5
  189.9 1.2 bitcast_add_fusion.5
  191.2 1.2 bitcast_add_fusion.5
  192.4 1.2 bitcast_add_fusion.5
  193.6 1.2 bitcast_add_fusion.5
  194.9 1.2 bitcast_add_fusion.5
  196.1 1.2 bitcast_add_fusion.5
  197.4 1.2 bitcast_add_fusion.5
  198.6 1.2 bitcast_add_fusion.5
  199.9 1.2 bitcast_add_fusion.5
  201.1 1.2 bitcast_add_fusion.5
  202.3 0.7 fusion.9
  203.0 0.4 fusion.13
  203.4 0.8 copy.85
  204.2 0.6 fusion.11
  204.8 0.4 fusion.12
  205.2 0.9 copy.86
  206.1 55.5 %all-gather.10.cloned.1.call-done = bf16[768,6144]{1,0:T(8,128)(2,1)} async-done(((bf16[48,6144]{1,0:T(8,128)(2,1)}), bf16[768,6144]{1,0:T(8,128)(2,1)}) %all-gather.10.cloned.1.call-update) | async-done | bytes 9437200 | tf_op jit(solution)/shard_map/all_gather | solution.py:95
  261.6 11.6 %multiply_reduce_fusion = (f32[768]{0:T(1024)S(1)}, bf16[1,768,576]{1,2,0:T(8,128)(2,1)}) fusion(bf16[1,768,576]{1,2,0:T(8,128)(2,1)} %param.22, f32[768]{0:T(1024)S(1)} %convert_element_type.83, bf16[768,6144]{1,0:T(8,128)(2,1)} %all-gather.10.cloned.1.call-done, bf16[1,576,6144]{2,1,0:T(8,128)(2,1)} %param.23), kind=kOutput, calls=%fused_computation.12 | convolution fusion | flops 5438028800 | bytes 18290688 | tf_op jit(solution)/shard_map/dot_general | solution.py:97
  273.2 31.2 %all-reduce.1 = f32[768]{0:T(1024)S(1)} all-reduce(f32[768]{0:T(1024)S(1)} %get-tuple-element.206), channel_id=4, replica_groups=mesh['seq'=16,'exp'=8] {'seq'}, use_global_device_ids=true, to_apply=%region_9.10.clone | all-reduce | flops 768 | bytes 6144
  304.5 20.6 %psum.7 = f32[128,2]{0,1:T(2,128)} all-reduce(f32[128,2]{0,1:T(2,128)S(1)} %broadcast_select_fusion), channel_id=1, replica_groups=mesh['seq'=16,'exp'=8] {'exp'}, use_global_device_ids=true, to_apply=%region_10.11 | all-reduce | flops 256 | bytes 2048 | tf_op jit(solution)/shard_map/psum | solution.py:112
  325.1 12.0 %fusion.3 = bf16[1,576,6144]{2,1,0:T(8,128)(2,1)} fusion(bf16[768,6144]{1,0:T(8,128)(2,1)} %all-gather.10.cloned.1.call-done, f32[768]{0:T(1024)S(1)} %convert_element_type.83, bf16[1,768,576]{1,2,0:T(8,128)(2,1)S(1)} %copy-done.2), kind=kOutput, calls=%fused_computation.8 | convolution fusion | flops 5453512704 | bytes 17402880 | tf_op jit(solution)/shard_map/dot_general | solution.py:105
  (48 shorter events, 1.6 us)
Async XLA Ops:
  7.2 3.0 copy-start
  7.2 33.4 %copy-start.1 = (u32[128]{0:T(128)S(1)}, u32[128]{0:T(128)}, u32[]{:S(2)}) copy-start(u32[128]{0:T(128)} %constant.81) | copy-start | bytes 1540
  7.2 30.7 %all-gather.8.cloned.1.call-start = ((), (), s32[]{:S(2)}) async-start(), calls=%async_computation | async-start | bytes 1769472 | tf_op jit(solution)/shard_map/all_gather | solution.py:89
  7.9 103.3 %all-gather.12.cloned.1.call-start = ((), (), s32[]{:S(2)}) async-start(), calls=%async_computation.2 | async-start | bytes 8912896 | tf_op jit(solution)/shard_map/all_gather | solution.py:13
  11.4 172.3 %all-gather.14.cloned.1.call-start = ((), (), s32[]{:S(2)}) async-start(), calls=%async_computation.3 | async-start | bytes 8912896 | tf_op jit(solution)/shard_map/all_gather | solution.py:13
  15.3 246.3 %all-gather.10.cloned.1.call-start = ((), (), s32[]{:S(2)}) async-start(), calls=%async_computation.1 | async-start | bytes 10027008 | tf_op jit(solution)/shard_map/all_gather | solution.py:95
  206.1 119.0 %copy-start.2 = (bf16[1,768,576]{1,2,0:T(8,128)(2,1)S(1)}, bf16[1,768,576]{1,2,0:T(8,128)(2,1)}, u32[]{:S(2)}) copy-start(bf16[1,768,576]{1,2,0:T(8,128)(2,1)} %param.22) | copy-start | bytes 2654212
Sparse Core Ops, SparseCore 0:
  9.7 28.1 all-gather.7
  40.6 70.5 all-gather.11
  113.4 70.2 all-gather.13
  186.2 75.2 all-gather.9
where the time goes:
time: 345 us; the launch traced here: 344 us
  waiting for transfers between devices  168 us (49%)
  blocking collectives  100 us (29%)
  matrix products  33 us (10%)
  other arithmetic  19.2 us (6%)
  between operations  15.2 us (4%)
  local copies, waits for them, and re-layouts  8.11 us (2%)
    all_gather x2, waiting for transfers between devices, prefix(): gathered = jax.tree.map(lambda a: lax.all_gather(a, axis), part)  89.8 us
    unnamed x2, blocking collectives  64.5 us
    all_gather x1, waiting for transfers between devices, on_device(): piece_rows = lax.all_gather(slot_rows, 'seq', axis=0, tiled=True)  55.5 us
    all_gather x1, waiting for transfers between devices, on_device(): whole_rows = lax.all_gather(moe_grad, 'exp', axis=1, tiled=True)  21.5 us
    psum x1, blocking collectives, on_device(): gate_grad = lax.psum(local_gate, 'exp')  20.6 us
    add x15, other arithmetic, chain_combine(): jnp.exp(latter[1])[:, None, None] * earlier[0] + latter[0]  17.9 us
    all_gather x1, blocking collectives, prefix(): gathered = jax.tree.map(lambda a: lax.all_gather(a, axis), part)  15 us
    dot_general x1, matrix products, on_device(): lax.dot_general(hidden_here, weighted, (((0,), (0,)), ((), ())), preferre...  12 us
  transfers between devices with their start and end apart: 4, of which 4 were waited for; matrix products, arithmetic and copies ran while one was open for 11% of the time, Pallas kernels for 0%

commit v1 on v0

--- a/solution.py
+++ b/solution.py
@@ -86,7 +86,11 @@
     slot_ids = jnp.arange(cap_size, dtype=jnp.int32)
     selector = ((slot_rank[None, :] == slot_ids[:, None]) & routed[None, :]).astype(jnp.float32)
     slot_gate = jnp.dot(selector, token_gate, precision=precise).astype(jnp.bfloat16)
-    whole_rows = lax.all_gather(moe_grad, "exp", axis=1, tiled=True)
+    size = lax.axis_size("exp")
+    repeats = [size if d == 1 else 1 for d in range(moe_grad.ndim)]
+    whole_rows = lax.all_to_all(
+        jnp.tile(moe_grad, repeats), "exp", split_axis=1, concat_axis=1, tiled=True
+    )
     slot_rows = jnp.dot(
         selector.astype(jnp.bfloat16), whole_rows, preferred_element_type=jnp.float32
     ).astype(jnp.bfloat16)

time: 345 us -> 319 us (0.925)
  waiting for transfers between devices: 168 us -> 133 us
  starting transfers between devices: 0.16 us -> 6.9 us
  local copies, waits for them, and re-layouts: 8.11 us -> 11.9 us
    all_gather x2, waiting for transfers between devices: 89.8 us -> 56.8 us  [prefix(): gathered = jax.tree.map(lambda a: lax.all_gather(a, axis), part)]
    all_gather x1 -> x0, waiting for transfers between devices: 21.5 us -> none  [on_device(): whole_rows = lax.all_gather(moe_grad, 'exp', axis=1, tiled=True)]
    all_to_all x0 -> x1, waiting for transfers between devices: none -> 20.3 us  [on_device(): lax.all_to_all(jnp.tile(moe_grad, repeats), 'exp', split_axis=1, concat_a...]
    all_to_all x0 -> x1, starting transfers between devices: none -> 6.81 us  [on_device(): lax.all_to_all(jnp.tile(moe_grad, repeats), 'exp', split_axis=1, concat_a...]
  transfers between devices with their start and end apart: 4 -> 4, of which waited for: 4 -> 3; matrix products, arithmetic and copies ran while one was open for 11% -> 11% of each run, Pallas kernels for 0% -> 0%
where the time goes in v1:
time: 319 us; the launch traced here: 317 us
  waiting for transfers between devices  133 us (42%)
  blocking collectives  98.9 us (31%)
  matrix products  32.8 us (10%)
  other arithmetic  18.5 us (6%)
  between operations  15.3 us (5%)
  local copies, waits for them, and re-layouts  11.9 us (4%)
  starting transfers between devices  6.9 us (2%)
    unnamed x2, blocking collectives  65.4 us
    all_gather x2, waiting for transfers between devices, prefix(): gathered = jax.tree.map(lambda a: lax.all_gather(a, axis), part)  56.8 us
    all_gather x1, waiting for transfers between devices, on_device(): piece_rows = lax.all_gather(slot_rows, 'seq', axis=0, tiled=True)  55.6 us
    psum x1, blocking collectives, on_device(): gate_grad = lax.psum(local_gate, 'exp')  20.6 us
    all_to_all x1, waiting for transfers between devices, on_device(): lax.all_to_all(jnp.tile(moe_grad, repeats), 'exp', split_axis=1, concat_a...  20.3 us
    add x15, other arithmetic, chain_combine(): jnp.exp(latter[1])[:, None, None] * earlier[0] + latter[0]  18 us
    all_gather x1, blocking collectives, prefix(): gathered = jax.tree.map(lambda a: lax.all_gather(a, axis), part)  13 us
    dot_general x1, matrix products, on_device(): lax.dot_general(piece_rows, weight_here, (((1,), (1,)), ((), ())), prefer...  11.6 us
  transfers between devices with their start and end apart: 4, of which 3 were waited for; matrix products, arithmetic and copies ran while one was open for 11% of the time, Pallas kernels for 0%

profile of v1, /device:TPU:1, one launch (start us, length us, event | category | flops | bytes accessed | tf_op | source)
XLA Modules:
  0.0 317.5 jit_solution(7576437686698565336)
XLA Ops:
  7.2 0.8 copy.89
  8.2 1.1 copy.92
  9.5 1.2 fusion.21
  10.8 1.1 copy.119
  11.9 1.1 copy.99
  13.1 1.4 fusion.18
  14.6 2.2 tile.2
  16.7 6.8 %all-to-all-start = ((bf16[128,8,768]{2,0,1:T(8,128)(2,1)}), bf16[128,8,768]{2,0,1:T(8,128)(2,1)S(1)}, u32[]{:S(2)}, u32[]{:S(2)}) async-start(bf16[128,8,768]{2,0,1:T(8,128)(2,1)} %tile.2), calls=%async_computation | async-start | bytes 3145728 | tf_op jit(solution)/shard_map/all_to_all | solution.py:91
  24.0 20.3 %all-to-all-done = bf16[128,8,768]{2,0,1:T(8,128)(2,1)S(1)} async-done(((bf16[128,8,768]{2,0,1:T(8,128)(2,1)}), bf16[128,8,768]{2,0,1:T(8,128)(2,1)S(1)}, u32[]{:S(2)}, u32[]{:S(2)}) %all-to-all-start) | async-done | bytes 1572896 | tf_op jit(solution)/shard_map/all_to_all | solution.py:91
  44.3 1.6 copy.109
  45.8 2.9 convolution_convert_fusion
  48.8 0.6 fusion.44
  50.2 0.2 dynamic-update-slice
  50.4 34.2 %all-reduce = bf16[768]{0:T(1024)(128)(2,1)S(1)} all-reduce(bf16[768]{0:T(1024)(128)(2,1)S(1)} %dynamic-update-slice), channel_id=1, replica_groups=mesh['seq'=16,'exp'=8] {'seq'}, use_global_device_ids=true, to_apply=%add | all-reduce | flops 768 | bytes 3072
  85.3 13.0 %all-gather.2 = f32[16,1,8]{2,1,0:T(1,128)S(1)} all-gather(f32[1,1,8]{2,1,0:T(1,128)S(1)} %get-tuple-element.227), channel_id=1, replica_groups=mesh['seq'=16,'exp'=8] {'seq'}, dimensions={0}, use_global_device_ids=true | all-gather | bytes 544 | tf_op jit(solution)/shard_map/all_gather | solution.py:13
  98.3 0.3 convolution_multiply_fusion.1
  98.6 0.3 convolution_multiply_fusion
  99.0 0.4 fusion.7
  99.4 0.7 fusion.14
  100.1 0.9 copy.110
  101.0 56.8 %all-gather.11.cloned.1.call-done = f32[128,128,128]{2,1,0:T(8,128)} async-done(((f32[8,128,128]{2,1,0:T(8,128)}), f32[128,128,128]{2,1,0:T(8,128)}) %all-gather.11.cloned.1.call-update) | async-done | bytes 8388624 | tf_op jit(solution)/shard_map/all_gather | solution.py:13
  157.8 18.6 %while.27 = (s32[]{:T(128)}, f32[8,128,128]{2,1,0:T(8,128)S(1)}, s32[]{:T(128)}, f32[16,8]{1,0:T(8,128)S(1)}, f32[16,8,128,128]{3,2,1,0:T(8,128)}, /*index=5*/s32[]{:T(128)}, s32[]{:T(128)}, s32[]{:T(128)}, s32[]{:T(128)}) while((s32[]{:T(128)}, f32[8,128,128]{2,1,0:T(8,128)S(1)}, s32[]{:T(128)}, f32[16,8]{1,0:T(8,128)S(1)}, ...), condition=%wide.region_4.5_spmd, body=%wide.region_3.4_spmd.sunk | while | flops 262150 | bytes 1573115 | solution.py:22
  157.9 1.2 bitcast_add_fusion.5
  159.1 1.2 bitcast_add_fusion.5
  160.3 1.2 bitcast_add_fusion.5
  161.6 1.2 bitcast_add_fusion.5
  162.8 1.2 bitcast_add_fusion.5
  164.0 1.2 bitcast_add_fusion.5
  165.3 1.2 bitcast_add_fusion.5
  166.5 1.2 bitcast_add_fusion.5
  167.7 1.2 bitcast_add_fusion.5
  169.0 1.2 bitcast_add_fusion.5
  170.2 1.2 bitcast_add_fusion.5
  171.5 1.2 bitcast_add_fusion.5
  172.8 1.2 bitcast_add_fusion.5
  174.0 1.2 bitcast_add_fusion.5
  175.2 1.2 bitcast_add_fusion.5
  176.4 0.7 fusion.9
  177.1 0.4 fusion.13
  177.5 0.9 copy.111
  178.4 0.6 fusion.11
  179.0 0.4 fusion.12
  179.4 0.8 copy.112
  180.2 55.6 %all-gather.7.cloned.1.call-done = bf16[768,6144]{1,0:T(8,128)(2,1)} async-done(((bf16[48,6144]{1,0:T(8,128)(2,1)}), bf16[768,6144]{1,0:T(8,128)(2,1)}) %all-gather.7.cloned.1.call-update) | async-done | bytes 9437200 | tf_op jit(solution)/shard_map/all_gather | solution.py:99
  235.8 11.6 %multiply_reduce_fusion = (f32[768]{0:T(1024)S(1)}, bf16[1,768,576]{1,2,0:T(8,128)(2,1)}) fusion(bf16[1,768,576]{1,2,0:T(8,128)(2,1)} %param.22, f32[768]{0:T(1024)S(1)} %convert_element_type.83, bf16[768,6144]{1,0:T(8,128)(2,1)} %all-gather.7.cloned.1.call-done, bf16[1,576,6144]{2,1,0:T(8,128)(2,1)} %param.23), kind=kOutput, calls=%fused_computation.12 | convolution fusion | flops 5438028800 | bytes 18290688 | tf_op jit(solution)/shard_map/dot_general | solution.py:101
  247.4 31.2 %all-reduce.1 = f32[768]{0:T(1024)S(1)} all-reduce(f32[768]{0:T(1024)S(1)} %get-tuple-element.222), channel_id=4, replica_groups=mesh['seq'=16,'exp'=8] {'seq'}, use_global_device_ids=true, to_apply=%region_9.10.clone | all-reduce | flops 768 | bytes 6144
  278.8 20.6 %psum.7 = f32[128,2]{0,1:T(2,128)} all-reduce(f32[128,2]{0,1:T(2,128)S(1)} %broadcast_select_fusion), channel_id=1, replica_groups=mesh['seq'=16,'exp'=8] {'exp'}, use_global_device_ids=true, to_apply=%region_10.11 | all-reduce | flops 256 | bytes 2048 | tf_op jit(solution)/shard_map/psum | solution.py:116
  299.4 11.6 %fusion.3 = bf16[1,576,6144]{2,1,0:T(8,128)(2,1)} fusion(bf16[768,6144]{1,0:T(8,128)(2,1)} %all-gather.7.cloned.1.call-done, f32[768]{0:T(1024)S(1)} %convert_element_type.83, bf16[1,768,576]{1,2,0:T(8,128)(2,1)S(1)} %copy-done.4), kind=kOutput, calls=%fused_computation.8 | convolution fusion | flops 5453512704 | bytes 17402880 | tf_op jit(solution)/shard_map/dot_general | solution.py:109
  (53 shorter events, 1.6 us)
Async XLA Ops:
  7.2 2.3 copy-start
  7.2 16.4 %copy-start.3 = (bf16[128,2]{0,1:T(2,128)(2,1)S(1)}, bf16[128,2]{0,1:T(2,128)(2,1)}, u32[]{:S(2)}) copy-start(bf16[128,2]{0,1:T(2,128)(2,1)} %param.20) | copy-start | bytes 1540
  7.2 16.4 %copy-start.2 = (s32[128,2]{0,1:T(2,128)S(1)}, s32[128,2]{0,1:T(2,128)}, u32[]{:S(2)}) copy-start(s32[128,2]{0,1:T(2,128)} %param.21) | copy-start | bytes 3076
  7.2 91.8 %all-gather.9.cloned.1.call-start = ((), (), s32[]{:S(2)}) async-start(), calls=%async_computation.2 | async-start | bytes 8912896 | tf_op jit(solution)/shard_map/all_gather | solution.py:13
  10.7 38.1 %copy-start.1 = (u32[128]{0:T(128)S(1)}, u32[128]{0:T(128)}, u32[]{:S(2)}) copy-start(u32[128]{0:T(128)} %constant.81) | copy-start | bytes 1540
  10.7 147.1 %all-gather.11.cloned.1.call-start = ((), (), s32[]{:S(2)}) async-start(), calls=%async_computation.3 | async-start | bytes 8912896 | tf_op jit(solution)/shard_map/all_gather | solution.py:13
  16.7 27.5 %all-to-all-start = ((bf16[128,8,768]{2,0,1:T(8,128)(2,1)}), bf16[128,8,768]{2,0,1:T(8,128)(2,1)S(1)}, u32[]{:S(2)}, u32[]{:S(2)}) async-start(bf16[128,8,768]{2,0,1:T(8,128)(2,1)} %tile.2), calls=%async_computation | async-start | bytes 3145728 | tf_op jit(solution)/shard_map/all_to_all | solution.py:91
  23.6 212.3 %all-gather.7.cloned.1.call-start = ((), (), s32[]{:S(2)}) async-start(), calls=%async_computation.1 | async-start | bytes 10027008 | tf_op jit(solution)/shard_map/all_gather | solution.py:99
  180.2 119.2 %copy-start.4 = (bf16[1,768,576]{1,2,0:T(8,128)(2,1)S(1)}, bf16[1,768,576]{1,2,0:T(8,128)(2,1)}, u32[]{:S(2)}) copy-start(bf16[1,768,576]{1,2,0:T(8,128)(2,1)} %param.22) | copy-start | bytes 2654212
Sparse Core Ops, SparseCore 0:
  10.8 74.4 all-gather.8
  87.4 70.2 all-gather.10
  160.5 75.2 all-gather.6
